TPU v7x, 256 devices: a whole 4x4x8 slice. The times are simulated.
256 devices in a mesh: seq: 16 (over x, y_hi, core), fsdp: 16 (over z, y_lo).
Axes of the slice: x: 4, y: 4 (y_hi: 2, y_lo: 2; y = y_hi * 2 + y_lo), z: 8, core: 2. Of those that a mesh axis runs over, the one named last changes fastest.
Arguments:
- hidden: bfloat16 [32768, 8192], P(('seq', 'fsdp')), may hold values from -24 to 24
- kv_blocks: bfloat16 [8192, 1024], P('fsdp'), may hold values from -0.0625 to 0.0625
- kv_scale: float32 [64, 8], P('fsdp'), may hold values from 0.5 to 2
- queries: bfloat16 [32768, 4096], P(('seq', 'fsdp')), may hold values from -24 to 24
- grad_out: bfloat16 [32768, 4096], P(('seq', 'fsdp')), may hold values from -6 to 6
Outputs:
- attn_out: bfloat16 [32768, 4096], P(('seq', 'fsdp'))
- grad_queries: bfloat16 [32768, 4096], P(('seq', 'fsdp'))
- grad_hidden: bfloat16 [32768, 8192], P(('seq', 'fsdp'))
- weight_grad: float32 [8192, 1024], P('fsdp')
All inputs are finite; a program needn't handle non-finite values.
Results may differ from a plain program's by a relative error of at most 0.0075.
The roundings to bfloat16 on the way count: a program that leaves them out, or rounds other values in their place, can miss the bound.
Values may be sent and summed in bfloat16 or wider, within the bound.
No kernel may reach another device: no remote copies, remote signals or barrier semaphores. Data moves between devices by JAX's collectives and lax.ppermute only.
A program may use at most 128 MiB of HBM per device.

v0:
```python
import jax
import jax.numpy as jnp
from jax import lax
from jax.sharding import Mesh
from jax.sharding import PartitionSpec as P

HEADS = 32
KV_HEADS = 4
HEAD = 128
QB = 128
FSDP = ("fsdp_0", "fsdp_1")
SEQ_FSDP = ("seq", "fsdp_0", "fsdp_1")
NEG = -1e30


def gather_axes(value, axes, dim):
    if not axes:
        return value
    nearer = lax.all_gather(value, axes[-1], axis=dim, tiled=True)
    return gather_axes(nearer, axes[:-1], dim)


def shifted(block, axis, distance):
    devices = range(lax.axis_size(axis))
    route = [(i - distance, i) for i in devices if i - distance in devices]
    return lax.ppermute(block, axis, route)


def dequantize(blocks, scale):
    rows, cols = blocks.shape
    grid = blocks.astype(jnp.float32).reshape(scale.shape[0], QB, scale.shape[1], QB)
    return (grid * scale[:, None, :, None]).reshape(rows, cols).astype(jnp.bfloat16)


def attend_group(operands, allowed):
    qgrp, kgrp, vgrp, ggrp = operands
    factor = 1.0 / float(HEAD) ** 0.5
    scores = jnp.einsum("rhd,kd->rhk", qgrp, kgrp, preferred_element_type=jnp.float32) * factor
    scores = jnp.where(allowed[:, None, :], scores, NEG)
    top = jnp.max(scores, axis=-1, keepdims=True)
    expd = jnp.exp(scores - top)
    probs = expd / jnp.sum(expd, axis=-1, keepdims=True)
    probs_b = probs.astype(jnp.bfloat16)
    output = jnp.einsum("rhk,kd->rhd", probs_b, vgrp, preferred_element_type=jnp.float32).astype(
        jnp.bfloat16
    )
    dprobs = jnp.einsum("rhd,kd->rhk", ggrp, vgrp, preferred_element_type=jnp.float32)
    delta = jnp.sum(probs * dprobs, axis=-1, keepdims=True)
    dscores = (probs * (dprobs - delta) * factor).astype(jnp.bfloat16)
    gradq = jnp.einsum("rhk,kd->rhd", dscores, kgrp, preferred_element_type=jnp.float32).astype(
        jnp.bfloat16
    )
    gradk = jnp.einsum("rhk,rhd->kd", dscores, qgrp, preferred_element_type=jnp.float32)
    gradv = jnp.einsum("rhk,rhd->kd", probs_b, ggrp, preferred_element_type=jnp.float32)
    return (output, gradq, gradk, gradv)


def attend(queries, window, grad_out, allowed):
    rows = queries.shape[0]
    count = window.shape[0]
    group = HEADS // KV_HEADS
    kvw = KV_HEADS * HEAD
    qgrp = queries.reshape(rows, KV_HEADS, group, HEAD).transpose(1, 0, 2, 3)
    ggrp = grad_out.reshape(rows, KV_HEADS, group, HEAD).transpose(1, 0, 2, 3)
    kgrp = window[:, :kvw].reshape(count, KV_HEADS, HEAD).transpose(1, 0, 2)
    vgrp = window[:, kvw:].reshape(count, KV_HEADS, HEAD).transpose(1, 0, 2)
    output, gradq, gradk, gradv = lax.map(
        lambda ops: attend_group(ops, allowed), (qgrp, kgrp, vgrp, ggrp)
    )
    output = output.transpose(1, 0, 2, 3).reshape(rows, HEADS * HEAD)
    gradq = gradq.transpose(1, 0, 2, 3).reshape(rows, HEADS * HEAD)
    gradk = gradk.transpose(1, 0, 2).reshape(count, kvw)
    gradv = gradv.transpose(1, 0, 2).reshape(count, kvw)
    return (output, gradq, jnp.concatenate([gradk, gradv], axis=1))


def body(hidden, kv_blocks, kv_scale, queries, grad_out):
    tok = hidden.shape[0]
    groups = lax.axis_size(FSDP)
    reach = groups // 2
    place = lax.axis_index(FSDP)
    linear = lax.axis_index("seq") * groups + place
    weights = dequantize(kv_blocks, kv_scale)
    columns = lax.all_to_all(hidden, FSDP, split_axis=1, concat_axis=0, tiled=True)
    whole = gather_axes(weights, FSDP, 0)
    kv = jnp.dot(hidden, whole, preferred_element_type=jnp.float32).astype(jnp.bfloat16)
    pieces = []
    for offset in range(reach, 0, -1):
        pieces.append(shifted(kv, SEQ_FSDP, offset))
    window = jnp.concatenate(pieces + [kv], axis=0)
    base = linear * tok
    qpos = base + jnp.arange(tok, dtype=jnp.int32)
    kpos = base - reach * tok + jnp.arange((reach + 1) * tok, dtype=jnp.int32)
    span = reach * tok
    allowed = (
        (qpos[:, None] - kpos[None, :] < span)
        & (kpos[None, :] <= qpos[:, None])
        & (kpos[None, :] >= 0)
    )
    attn_out, grad_queries, dwin = attend(queries, window, grad_out, allowed)
    total = dwin[reach * tok :]
    inside = total
    for offset in range(1, reach + 1):
        piece = dwin[(reach - offset) * tok : (reach - offset + 1) * tok]
        returned = shifted(piece, SEQ_FSDP, -offset)
        total = total + returned
        inside = inside + jnp.where(place + offset < groups, returned, jnp.zeros_like(returned))
    all_grad = total.astype(jnp.bfloat16)
    seg_grad = inside.astype(jnp.bfloat16)
    grad_hidden = lax.dot_general(
        seg_grad, whole, (((1,), (1,)), ((), ())), preferred_element_type=jnp.float32
    ).astype(jnp.bfloat16)
    shard_grad = lax.dot_general(
        columns,
        lax.all_gather(all_grad, FSDP, axis=0, tiled=True),
        (((0,), (0,)), ((), ())),
        preferred_element_type=jnp.float32,
    )
    weight_grad = lax.psum(shard_grad, "seq")
    return (attn_out, grad_queries, grad_hidden, weight_grad)


def solution(mesh):
    finer = Mesh(mesh.devices.reshape(mesh.shape["seq"], 8, 2), ("seq", "fsdp_0", "fsdp_1"))
    placed = (P(SEQ_FSDP, None), P(FSDP, None), P(FSDP, None), P(SEQ_FSDP, None), P(SEQ_FSDP, None))
    return jax.shard_map(
        body,
        mesh=finer,
        in_specs=placed,
        out_specs=(P(SEQ_FSDP, None), P(SEQ_FSDP, None), P(SEQ_FSDP, None), P(FSDP, None)),
        check_vma=False,
    )
```

profile of v0, /device:TPU:1, one launch (start us, length us, event | category | flops | bytes accessed | tf_op | source)
XLA Modules:
  0.0 1012.2 jit_solution(2476808071577137936)
XLA Ops:
  10.0 42.4 %all-gather.4.cloned.1.call-done = bf16[1024,1024]{1,0:T(8,128)(2,1)} async-done(((bf16[512,1024]{1,0:T(8,128)(2,1)}), bf16[1024,1024]{1,0:T(8,128)(2,1)}) %all-gather.4.cloned.1.call-update) | async-done | bytes 2097168 | tf_op jit(solution)/shard_map/all_gather | solution.py:19
  52.5 175.5 %all-gather.6.cloned.1.call-done = bf16[8192,1024]{1,0:T(8,128)(2,1)} async-done(((bf16[1024,1024]{1,0:T(8,128)(2,1)}), bf16[8192,1024]{1,0:T(8,128)(2,1)}) %all-gather.6.cloned.1.call-update) | async-done | bytes 16777232 | tf_op jit(solution)/shard_map/all_gather | solution.py:19
  228.0 8.1 fusion.100
  245.0 5.8 collective-permute-start.2
  271.7 18.8 %collective-permute-done.2 = bf16[128,1024]{1,0:T(8,128)(2,1)S(1)} collective-permute-done((bf16[128,1024]{1,0:T(8,128)(2,1)S(1)}, bf16[128,1024]{1,0:T(8,128)(2,1)S(1)}, u32[]{:S(2)}, u32[]{:S(2)}) %collective-permute-start.2) | collective-permute-done | bytes 262176 | tf_op jit(solution)/shard_map/ppermute | solution.py:26
  292.5 13.1 %collective-permute-done.3 = bf16[128,1024]{1,0:T(8,128)(2,1)S(1)} collective-permute-done((bf16[128,1024]{1,0:T(8,128)(2,1)S(1)}, bf16[128,1024]{1,0:T(8,128)(2,1)S(1)}, u32[]{:S(2)}, u32[]{:S(2)}) %collective-permute-start.3) | collective-permute-done | bytes 262176 | tf_op jit(solution)/shard_map/ppermute | solution.py:26
  305.6 7.8 collective-permute-done.5
  313.4 8.5 collective-permute-done.6
  321.9 12.2 %collective-permute-done.7 = bf16[128,1024]{1,0:T(8,128)(2,1)S(1)} collective-permute-done((bf16[128,1024]{1,0:T(8,128)(2,1)S(1)}, bf16[128,1024]{1,0:T(8,128)(2,1)S(1)}, u32[]{:S(2)}, u32[]{:S(2)}) %collective-permute-start.7) | collective-permute-done | bytes 262176 | tf_op jit(solution)/shard_map/ppermute | solution.py:26
  336.1 180.6 %while.17 = (s32[]{:T(128)}, bf16[4,128,8,128]{3,1,2,0:T(8,128)(2,1)}, bf16[4,128,8,128]{3,1,2,0:T(8,128)(2,1)}, f32[4,1152,128]{1,2,0:T(8,128)S(1)}, f32[4,1152...) while((s32[]{:T(128)}, ...), condition=%wide.region_4.5_spmd.clone, body=%wide.region_0.4_spmd.clone.sunk | while | flops 2449958400 | bytes 52865276 | solution.py:67
  346.7 12.1 %fusion.171 = f32[4,1152,128]{1,2,0:T(8,128)S(1)} fusion(f32[4,1152,128]{1,2,0:T(8,128)S(1)} %get-tuple-element.259, s32[]{:T(128)} %get-tuple-element.256, f32[128,8,1152]{2,0,1:T(8,128)} %fusion.169, bf16[4,128,8,128]{1,3,2,0:T(8,128)(2,1)} %get-tuple-element.274, f32[128,8,1152]{2,0,1:T(8,128)} %get-tuple-element.242, ...), kind=kOutput, calls=%fused_computation.17.clone.1 | convolution fusion | flops 310249600 | bytes 19735552 | tf_op jit(solution)/shard_map/while/body/eval_jaxpr/rhk,rhd->kd/dot_general | solution.py:53
  358.7 12.5 %fusion.170 = bf16[4,128,8,128]{3,1,2,0:T(8,128)(2,1)} fusion(bf16[4,128,8,128]{3,1,2,0:T(8,128)(2,1)} %get-tuple-element.258, s32[]{:T(128)} %get-tuple-element.256, f32[128,8,1152]{2,0,1:T(8,128)} %fusion.169, bf16[4,1152,128]{2,1,0:T(8,128)(2,1)} %get-tuple-element.275, f32[128,8,1152]{2,0,1:T(8,128)} %get-tuple-element.242, ...), kind=kOutput, calls=%fused_computation.28.clone.1 | convolution fusion | flops 310380672 | bytes 19440640 | tf_op jit(solution)/shard_map/while/body/eval_jaxpr/rhk,kd->rhd/dot_general | solution.py:50
  382.1 5.7 exponential_reduce_fusion.2
  391.8 12.1 %fusion.171 = f32[4,1152,128]{1,2,0:T(8,128)S(1)} fusion(f32[4,1152,128]{1,2,0:T(8,128)S(1)} %get-tuple-element.259, s32[]{:T(128)} %get-tuple-element.256, f32[128,8,1152]{2,0,1:T(8,128)} %fusion.169, bf16[4,128,8,128]{1,3,2,0:T(8,128)(2,1)} %get-tuple-element.274, f32[128,8,1152]{2,0,1:T(8,128)} %get-tuple-element.242, ...), kind=kOutput, calls=%fused_computation.17.clone.1 | convolution fusion | flops 310249600 | bytes 19735552 | tf_op jit(solution)/shard_map/while/body/eval_jaxpr/rhk,rhd->kd/dot_general | solution.py:53
  403.9 12.5 %fusion.170 = bf16[4,128,8,128]{3,1,2,0:T(8,128)(2,1)} fusion(bf16[4,128,8,128]{3,1,2,0:T(8,128)(2,1)} %get-tuple-element.258, s32[]{:T(128)} %get-tuple-element.256, f32[128,8,1152]{2,0,1:T(8,128)} %fusion.169, bf16[4,1152,128]{2,1,0:T(8,128)(2,1)} %get-tuple-element.275, f32[128,8,1152]{2,0,1:T(8,128)} %get-tuple-element.242, ...), kind=kOutput, calls=%fused_computation.28.clone.1 | convolution fusion | flops 310380672 | bytes 19440640 | tf_op jit(solution)/shard_map/while/body/eval_jaxpr/rhk,kd->rhd/dot_general | solution.py:50
  437.0 12.1 %fusion.171 = f32[4,1152,128]{1,2,0:T(8,128)S(1)} fusion(f32[4,1152,128]{1,2,0:T(8,128)S(1)} %get-tuple-element.259, s32[]{:T(128)} %get-tuple-element.256, f32[128,8,1152]{2,0,1:T(8,128)} %fusion.169, bf16[4,128,8,128]{1,3,2,0:T(8,128)(2,1)} %get-tuple-element.274, f32[128,8,1152]{2,0,1:T(8,128)} %get-tuple-element.242, ...), kind=kOutput, calls=%fused_computation.17.clone.1 | convolution fusion | flops 310249600 | bytes 19735552 | tf_op jit(solution)/shard_map/while/body/eval_jaxpr/rhk,rhd->kd/dot_general | solution.py:53
  449.0 12.5 %fusion.170 = bf16[4,128,8,128]{3,1,2,0:T(8,128)(2,1)} fusion(bf16[4,128,8,128]{3,1,2,0:T(8,128)(2,1)} %get-tuple-element.258, s32[]{:T(128)} %get-tuple-element.256, f32[128,8,1152]{2,0,1:T(8,128)} %fusion.169, bf16[4,1152,128]{2,1,0:T(8,128)(2,1)} %get-tuple-element.275, f32[128,8,1152]{2,0,1:T(8,128)} %get-tuple-element.242, ...), kind=kOutput, calls=%fused_computation.28.clone.1 | convolution fusion | flops 310380672 | bytes 19440640 | tf_op jit(solution)/shard_map/while/body/eval_jaxpr/rhk,kd->rhd/dot_general | solution.py:50
  472.4 5.7 exponential_reduce_fusion.2
  482.1 12.1 %fusion.171 = f32[4,1152,128]{1,2,0:T(8,128)S(1)} fusion(f32[4,1152,128]{1,2,0:T(8,128)S(1)} %get-tuple-element.259, s32[]{:T(128)} %get-tuple-element.256, f32[128,8,1152]{2,0,1:T(8,128)} %fusion.169, bf16[4,128,8,128]{1,3,2,0:T(8,128)(2,1)} %get-tuple-element.274, f32[128,8,1152]{2,0,1:T(8,128)} %get-tuple-element.242, ...), kind=kOutput, calls=%fused_computation.17.clone.1 | convolution fusion | flops 310249600 | bytes 19735552 | tf_op jit(solution)/shard_map/while/body/eval_jaxpr/rhk,rhd->kd/dot_general | solution.py:53
  494.2 12.5 %fusion.170 = bf16[4,128,8,128]{3,1,2,0:T(8,128)(2,1)} fusion(bf16[4,128,8,128]{3,1,2,0:T(8,128)(2,1)} %get-tuple-element.258, s32[]{:T(128)} %get-tuple-element.256, f32[128,8,1152]{2,0,1:T(8,128)} %fusion.169, bf16[4,1152,128]{2,1,0:T(8,128)(2,1)} %get-tuple-element.275, f32[128,8,1152]{2,0,1:T(8,128)} %get-tuple-element.242, ...), kind=kOutput, calls=%fused_computation.28.clone.1 | convolution fusion | flops 310380672 | bytes 19440640 | tf_op jit(solution)/shard_map/while/body/eval_jaxpr/rhk,kd->rhd/dot_general | solution.py:50
  525.2 5.8 collective-permute-start.12
  536.8 17.9 %collective-permute-start.15 = (f32[128,1024]{0,1:T(8,128)S(1)}, f32[128,1024]{0,1:T(8,128)S(1)}, u32[]{:S(2)}, u32[]{:S(2)}) collective-permute-start(f32[128,1024]{0,1:T(8,128)S(1)} %get-tuple-element.160), channel_id=1, source_target_pairs={{8,0},{9,1},{10,2},{11,3},{12,4},{13,5},{14,6},{15,7},{16,8},{17,9... | collective-permute-start | bytes 1572872 | tf_op jit(solution)/shard_map/ppermute | solution.py:26
  554.7 15.7 %collective-permute-done.11 = f32[128,1024]{0,1:T(8,128)S(1)} collective-permute-done((f32[128,1024]{0,1:T(8,128)S(1)}, f32[128,1024]{0,1:T(8,128)S(1)}, u32[]{:S(2)}, u32[]{:S(2)}) %collective-permute-start.11) | collective-permute-done | bytes 524320 | tf_op jit(solution)/shard_map/ppermute | solution.py:26
  570.5 17.8 %collective-permute-start.8 = (f32[128,1024]{0,1:T(8,128)S(1)}, f32[128,1024]{0,1:T(8,128)S(1)}, u32[]{:S(2)}, u32[]{:S(2)}) collective-permute-start(f32[128,1024]{0,1:T(8,128)S(1)} %get-tuple-element.154), channel_id=1, source_target_pairs={{1,0},{2,1},{3,2},{4,3},{5,4},{6,5},{7,6},{8,7},{9,8},{10,9},{11,1... | collective-permute-start | bytes 1572872 | tf_op jit(solution)/shard_map/ppermute | solution.py:26
  588.3 13.7 %collective-permute-start.9 = (f32[128,1024]{0,1:T(8,128)S(1)}, f32[128,1024]{0,1:T(8,128)S(1)}, u32[]{:S(2)}, u32[]{:S(2)}) collective-permute-start(f32[128,1024]{0,1:T(8,128)S(1)} %get-tuple-element.155), channel_id=1, source_target_pairs={{2,0},{3,1},{4,2},{5,3},{6,4},{7,5},{8,6},{9,7},{10,8},{11,9},{12,... | collective-permute-start | bytes 1572872 | tf_op jit(solution)/shard_map/ppermute | solution.py:26
  602.0 32.7 %collective-permute-done.13 = f32[128,1024]{0,1:T(8,128)S(1)} collective-permute-done((f32[128,1024]{0,1:T(8,128)S(1)}, f32[128,1024]{0,1:T(8,128)S(1)}, u32[]{:S(2)}, u32[]{:S(2)}) %collective-permute-start.13) | collective-permute-done | bytes 524320 | tf_op jit(solution)/shard_map/ppermute | solution.py:26
  634.7 7.5 collective-permute-done.14
  649.5 131.0 %all_to_all.19 = bf16[128,16,512]{0,2,1:T(8,128)(2,1)} all-to-all(bf16[128,16,512]{0,2,1:T(8,128)(2,1)} %bitcast.168), channel_id=1, replica_groups=mesh['seq'=16,'fsdp_0'=8,'fsdp_1'=2] {'fsdp_0','fsdp_1'}, dimensions={1} | all-to-all | bytes 4194304 | tf_op jit(solution)/shard_map/all_to_all | solution.py:84
  784.4 56.0 %all-gather.8.cloned.1.call-done = bf16[2048,1024]{0,1:T(8,128)(2,1)} async-done(((bf16[128,1024]{0,1:T(8,128)(2,1)}), bf16[2048,1024]{0,1:T(8,128)(2,1)}) %all-gather.8.cloned.1.call-update) | async-done | bytes 4194320 | tf_op jit(solution)/shard_map/all_gather | solution.py:115
  840.5 6.5 convolution_bitcast_fusion.2
  852.6 13.9 %convolution_convert_fusion.1 = bf16[128,8192]{1,0:T(8,128)(2,1)} fusion(bf16[8192,1024]{1,0:T(8,128)(2,1)} %all-gather.6.cloned.1.call-done, f32[128,1024]{0,1:T(8,128)} %copy-done.5, f32[128,1024]{0,1:T(8,128)} %copy-done.4, f32[128,1024]{0,1:T(8,128)} %copy-done.3, f32[128,1024]{0,1:T(8,128)} %copy-done.2, f32[128,1024]{0,1:T(8,128)S(1)} %collective-permute-done.11, ...), kind=kOutput, calls=%fused_computation.83 | convolution fusion | flops 2150891520 | bytes 27787272 | tf_op jit(solution)/shard_map/dot_general | solution.py:110
  866.5 136.3 %all-reduce.2.cloned.1.call-done = f32[512,1024]{0,1:T(8,128)} async-done(((f32[512,1024]{0,1:T(8,128)}), f32[512,1024]{0,1:T(8,128)}) %all-reduce.2.cloned.1.call-update) | async-done | bytes 2097168 | tf_op jit(solution)/shard_map/psum | solution.py:119
  (96 shorter events, 140.9 us)
Async XLA Ops:
  7.2 1.2 copy-start.9
  7.2 45.2 %all-gather.4.cloned.1.call-start = ((), (), s32[]{:S(2)}) async-start(), calls=%async_computation.1 | async-start | bytes 3145728 | tf_op jit(solution)/shard_map/all_gather | solution.py:19
  10.0 218.0 %copy-start.1 = (bf16[128,8192]{1,0:T(8,128)(2,1)S(1)}, bf16[128,8192]{1,0:T(8,128)(2,1)}, u32[]{:S(2)}) copy-start(bf16[128,8192]{1,0:T(8,128)(2,1)} %param.7) | copy-start | bytes 6291460
  10.0 218.0 %all-gather.6.cloned.1.call-start = ((), (), s32[]{:S(2)}) async-start(), calls=%async_computation.2 | async-start | bytes 18874368 | tf_op jit(solution)/shard_map/all_gather | solution.py:19
  52.4 788.0 %all-gather.8.cloned.1.call-start = ((), (), s32[]{:S(2)}) async-start(), calls=%async_computation.3 | async-start | bytes 4456448 | tf_op jit(solution)/shard_map/all_gather | solution.py:115
  236.1 26.6 %collective-permute-start = (bf16[128,1024]{1,0:T(8,128)(2,1)S(1)}, bf16[128,1024]{1,0:T(8,128)(2,1)}, u32[]{:S(2)}, u32[]{:S(2)}) collective-permute-start(bf16[128,1024]{1,0:T(8,128)(2,1)S(1)} %fusion.100), channel_id=1, source_target_pairs={{0,8},{1,9},{2,10},{3,11},{4,12},{5,13},{6,14},{7,15},{8,16},{9,17... | collective-permute-start | bytes 786440 | tf_op jit(solution)/shard_map/ppermute | solution.py:26
  240.8 28.2 %collective-permute-start.1 = (bf16[128,1024]{1,0:T(8,128)(2,1)S(1)}, bf16[128,1024]{1,0:T(8,128)(2,1)S(1)}, u32[]{:S(2)}, u32[]{:S(2)}) collective-permute-start(bf16[128,1024]{1,0:T(8,128)(2,1)S(1)} %fusion.100), channel_id=1, source_target_pairs={{0,7},{1,8},{2,9},{3,10},{4,11},{5,12},{6,13},{7,14},{8,15},{9,16}... | collective-permute-start | bytes 786440 | tf_op jit(solution)/shard_map/ppermute | solution.py:26
  245.0 45.6 %collective-permute-start.2 = (bf16[128,1024]{1,0:T(8,128)(2,1)S(1)}, bf16[128,1024]{1,0:T(8,128)(2,1)S(1)}, u32[]{:S(2)}, u32[]{:S(2)}) collective-permute-start(bf16[128,1024]{1,0:T(8,128)(2,1)S(1)} %fusion.100), channel_id=1, source_target_pairs={{0,6},{1,7},{2,8},{3,9},{4,10},{5,11},{6,12},{7,13},{8,14},{9,15},... | collective-permute-start | bytes 786440 | tf_op jit(solution)/shard_map/ppermute | solution.py:26
  255.4 50.2 %collective-permute-start.3 = (bf16[128,1024]{1,0:T(8,128)(2,1)S(1)}, bf16[128,1024]{1,0:T(8,128)(2,1)S(1)}, u32[]{:S(2)}, u32[]{:S(2)}) collective-permute-start(bf16[128,1024]{1,0:T(8,128)(2,1)S(1)} %fusion.100), channel_id=1, source_target_pairs={{0,5},{1,6},{2,7},{3,8},{4,9},{5,10},{6,11},{7,12},{8,13},{9,14},{... | collective-permute-start | bytes 786440 | tf_op jit(solution)/shard_map/ppermute | solution.py:26
  260.3 45.2 %collective-permute-start.4 = (bf16[128,1024]{1,0:T(8,128)(2,1)S(1)}, bf16[128,1024]{1,0:T(8,128)(2,1)S(1)}, u32[]{:S(2)}, u32[]{:S(2)}) collective-permute-start(bf16[128,1024]{1,0:T(8,128)(2,1)S(1)} %fusion.100), channel_id=1, source_target_pairs={{0,4},{1,5},{2,6},{3,7},{4,8},{5,9},{6,10},{7,11},{8,12},{9,13},{1... | collective-permute-start | bytes 786440 | tf_op jit(solution)/shard_map/ppermute | solution.py:26
  262.7 50.7 %collective-permute-start.5 = (bf16[128,1024]{1,0:T(8,128)(2,1)S(1)}, bf16[128,1024]{1,0:T(8,128)(2,1)S(1)}, u32[]{:S(2)}, u32[]{:S(2)}) collective-permute-start(bf16[128,1024]{1,0:T(8,128)(2,1)S(1)} %fusion.100), channel_id=1, source_target_pairs={{0,3},{1,4},{2,5},{3,6},{4,7},{5,8},{6,9},{7,10},{8,11},{9,12},{10... | collective-permute-start | bytes 786440 | tf_op jit(solution)/shard_map/ppermute | solution.py:26
  269.0 52.8 %collective-permute-start.6 = (bf16[128,1024]{1,0:T(8,128)(2,1)S(1)}, bf16[128,1024]{1,0:T(8,128)(2,1)S(1)}, u32[]{:S(2)}, u32[]{:S(2)}) collective-permute-start(bf16[128,1024]{1,0:T(8,128)(2,1)S(1)} %fusion.100), channel_id=1, source_target_pairs={{0,2},{1,3},{2,4},{3,5},{4,6},{5,7},{6,8},{7,9},{8,10},{9,11},{10,... | collective-permute-start | bytes 786440 | tf_op jit(solution)/shard_map/ppermute | solution.py:26
  290.5 43.6 %collective-permute-start.7 = (bf16[128,1024]{1,0:T(8,128)(2,1)S(1)}, bf16[128,1024]{1,0:T(8,128)(2,1)S(1)}, u32[]{:S(2)}, u32[]{:S(2)}) collective-permute-start(bf16[128,1024]{1,0:T(8,128)(2,1)S(1)} %fusion.100), channel_id=1, source_target_pairs={{0,1},{1,2},{2,3},{3,4},{4,5},{5,6},{6,7},{7,8},{8,9},{9,10},{10,1... | collective-permute-start | bytes 786440 | tf_op jit(solution)/shard_map/ppermute | solution.py:26
  516.7 127.6 %copy-start = (f32[4,1152,128]{1,2,0:T(8,128)S(1)}, f32[4,1152,128]{1,2,0:T(8,128)}, u32[]{:S(2)}) copy-start(f32[4,1152,128]{1,2,0:T(8,128)} %get-tuple-element.62) | copy-start | bytes 7077892
  518.7 18.1 %collective-permute-start.10 = (f32[128,1024]{0,1:T(8,128)S(1)}, f32[128,1024]{0,1:T(8,128)S(1)}, u32[]{:S(2)}, u32[]{:S(2)}) collective-permute-start(f32[128,1024]{0,1:T(8,128)S(1)} %get-tuple-element.156), channel_id=1, source_target_pairs={{3,0},{4,1},{5,2},{6,3},{7,4},{8,5},{9,6},{10,7},{11,8},{12,9},{13... | collective-permute-start | bytes 1572872 | tf_op jit(solution)/shard_map/ppermute | solution.py:26
  520.6 49.9 %collective-permute-start.11 = (f32[128,1024]{0,1:T(8,128)S(1)}, f32[128,1024]{0,1:T(8,128)S(1)}, u32[]{:S(2)}, u32[]{:S(2)}) collective-permute-start(f32[128,1024]{0,1:T(8,128)S(1)} %get-tuple-element.157), channel_id=1, source_target_pairs={{4,0},{5,1},{6,2},{7,3},{8,4},{9,5},{10,6},{11,7},{12,8},{13,9},{1... | collective-permute-start | bytes 1572872 | tf_op jit(solution)/shard_map/ppermute | solution.py:26
  525.2 63.1 %collective-permute-start.12 = (f32[128,1024]{0,1:T(8,128)S(1)}, f32[128,1024]{0,1:T(8,128)S(1)}, u32[]{:S(2)}, u32[]{:S(2)}) collective-permute-start(f32[128,1024]{0,1:T(8,128)S(1)} %get-tuple-element.158), channel_id=1, source_target_pairs={{5,0},{6,1},{7,2},{8,3},{9,4},{10,5},{11,6},{12,7},{13,8},{14,9},{... | collective-permute-start | bytes 1572872 | tf_op jit(solution)/shard_map/ppermute | solution.py:26
  531.0 103.8 %collective-permute-start.13 = (f32[128,1024]{0,1:T(8,128)S(1)}, f32[128,1024]{0,1:T(8,128)S(1)}, u32[]{:S(2)}, u32[]{:S(2)}) collective-permute-start(f32[128,1024]{0,1:T(8,128)S(1)} %get-tuple-element.159), channel_id=1, source_target_pairs={{6,0},{7,1},{8,2},{9,3},{10,4},{11,5},{12,6},{13,7},{14,8},{15,9},... | collective-permute-start | bytes 1572872 | tf_op jit(solution)/shard_map/ppermute | solution.py:26
  533.0 109.3 %collective-permute-start.14 = (f32[128,1024]{0,1:T(8,128)S(1)}, f32[128,1024]{0,1:T(8,128)S(1)}, u32[]{:S(2)}, u32[]{:S(2)}) collective-permute-start(f32[128,1024]{0,1:T(8,128)S(1)} %get-tuple-element.161), channel_id=1, source_target_pairs={{7,0},{8,1},{9,2},{10,3},{11,4},{12,5},{13,6},{14,7},{15,8},{16,9}... | collective-permute-start | bytes 1572872 | tf_op jit(solution)/shard_map/ppermute | solution.py:26
  536.8 105.5 %collective-permute-start.15 = (f32[128,1024]{0,1:T(8,128)S(1)}, f32[128,1024]{0,1:T(8,128)S(1)}, u32[]{:S(2)}, u32[]{:S(2)}) collective-permute-start(f32[128,1024]{0,1:T(8,128)S(1)} %get-tuple-element.160), channel_id=1, source_target_pairs={{8,0},{9,1},{10,2},{11,3},{12,4},{13,5},{14,6},{15,7},{16,8},{17,9... | collective-permute-start | bytes 1572872 | tf_op jit(solution)/shard_map/ppermute | solution.py:26
  570.5 71.8 %collective-permute-start.8 = (f32[128,1024]{0,1:T(8,128)S(1)}, f32[128,1024]{0,1:T(8,128)S(1)}, u32[]{:S(2)}, u32[]{:S(2)}) collective-permute-start(f32[128,1024]{0,1:T(8,128)S(1)} %get-tuple-element.154), channel_id=1, source_target_pairs={{1,0},{2,1},{3,2},{4,3},{5,4},{6,5},{7,6},{8,7},{9,8},{10,9},{11,1... | collective-permute-start | bytes 1572872 | tf_op jit(solution)/shard_map/ppermute | solution.py:26
  588.3 54.0 %copy-start.2 = (f32[128,1024]{0,1:T(8,128)}, f32[128,1024]{0,1:T(8,128)S(1)}, u32[]{:S(2)}) copy-start(f32[128,1024]{0,1:T(8,128)S(1)} %collective-permute-done.12) | copy-start | bytes 1572868
  588.3 54.0 %collective-permute-start.9 = (f32[128,1024]{0,1:T(8,128)S(1)}, f32[128,1024]{0,1:T(8,128)S(1)}, u32[]{:S(2)}, u32[]{:S(2)}) collective-permute-start(f32[128,1024]{0,1:T(8,128)S(1)} %get-tuple-element.155), channel_id=1, source_target_pairs={{2,0},{3,1},{4,2},{5,3},{6,4},{7,5},{8,6},{9,7},{10,8},{11,9},{12,... | collective-permute-start | bytes 1572872 | tf_op jit(solution)/shard_map/ppermute | solution.py:26
  634.7 7.6 copy-start.3
  642.3 0.8 copy-start.4
  642.3 1.0 copy-start.5
  642.3 1.2 copy-start.6
  643.5 0.8 copy-start.7
  645.4 357.4 %all-reduce.2.cloned.1.call-start = ((), (), s32[]{:S(2)}) async-start(), calls=%async_computation.4 | async-start | bytes 4194304 | tf_op jit(solution)/shard_map/psum | solution.py:119
  847.0 3.4 copy-start.8
Sparse Core Ops, SparseCore 0:
  10.4 41.9 all-gather.3
  54.2 173.7 all-gather.5
  645.5 194.9 all-gather.7
  847.1 155.5 all-reduce.1
where the time goes:
time: 1010 us
  waiting for transfers between devices  529 us (52%)
  matrix products  206 us (20%)
  blocking collectives  131 us (13%)
  starting transfers between devices  97.6 us (10%)
  local copies, waits for them, and re-layouts  27.1 us (3%)
  between operations  14.2 us (1%)
    all_gather x2, waiting for transfers between devices, gather_axes(): nearer = lax.all_gather(value, axes[-1], axis=dim, tiled=True)  218 us
    psum x1, waiting for transfers between devices, body(): weight_grad = lax.psum(shard_grad, 'seq')  136 us
    all_to_all x1, blocking collectives, body(): lax.all_to_all(hidden, FSDP, split_axis=1, concat_axis=0, tiled=True)  131 us
    ppermute x16, waiting for transfers between devices, shifted(): return lax.ppermute(block, axis, route)  118 us
    ppermute x16, starting transfers between devices, shifted(): return lax.ppermute(block, axis, route)  97.5 us
    all_gather x1, waiting for transfers between devices, body(): lax.all_gather(all_grad, FSDP, axis=0, tiled=True)  56 us
    dot_general x4, matrix products, attend_group(): jnp.einsum('rhk,kd->rhd', dscores, kgrp, preferred_element_type=jnp.float32)  50.1 us
    dot_general x4, matrix products, attend_group(): jnp.einsum('rhk,rhd->kd', dscores, qgrp, preferred_element_type=jnp.float32)  48.3 us
  transfers between devices with their start and end apart: 20, of which 13 were waited for; matrix products, arithmetic and copies ran while one was open for 3% of the time, Pallas kernels for 0%

commit v1 on v0

--- a/solution.py
+++ b/solution.py
@@ -3,6 +3,7 @@
 from jax import lax
 from jax.sharding import Mesh
 from jax.sharding import PartitionSpec as P
+from jax.lax import all_gather
 
 HEADS = 32
 KV_HEADS = 4
@@ -116,7 +117,12 @@
         (((0,), (0,)), ((), ())),
         preferred_element_type=jnp.float32,
     )
-    weight_grad = lax.psum(shard_grad, "seq")
+
+    def hubs_edit(field_in):
+        o_now = all_gather(field_in, "seq")
+        return jnp.sum(o_now, 0)
+
+    weight_grad = hubs_edit(shard_grad)
     return (attn_out, grad_queries, grad_hidden, weight_grad)
 
 

time: 1010 us -> 1110 us (1.099); the launches traced: 1010 us -> 1100 us
  waiting for transfers between devices: 529 us -> 596 us
  local copies, waits for them, and re-layouts: 27.1 us -> 60.9 us
  blocking collectives: 131 us -> 112 us
    all_gather x0 -> x1, waiting for transfers between devices: none -> 182 us  [hubs_edit(): o_now = all_gather(field_in, 'seq')]
    psum x1 -> x0, waiting for transfers between devices: 136 us -> none  [body(): weight_grad = lax.psum(shard_grad, 'seq')]
    unnamed x35 -> x36, local copies, waits for them, and re-layouts: 18 us -> 51.9 us
    ppermute x16, waiting for transfers between devices: 118 us -> 143 us  [shifted(): return lax.ppermute(block, axis, route)]
    all_to_all x1, blocking collectives: 131 us -> 112 us  [body(): lax.all_to_all(hidden, FSDP, split_axis=1, concat_axis=0, tiled=True)]
  transfers between devices with their start and end apart: 20 -> 20, of which waited for: 13 -> 12; matrix products, arithmetic and copies ran while one was open for 3% -> 3% of each run, Pallas kernels for 0% -> 0%
where the time goes in v1:
time: 1110 us; the launch traced here: 1100 us
  waiting for transfers between devices  596 us (54%)
  matrix products  206 us (19%)
  blocking collectives  112 us (10%)
  starting transfers between devices  93.6 us (8%)
  local copies, waits for them, and re-layouts  60.9 us (5%)
  other arithmetic  16.4 us (1%)
  between operations  14.4 us (1%)
    all_gather x2, waiting for transfers between devices, gather_axes(): nearer = lax.all_gather(value, axes[-1], axis=dim, tiled=True)  218 us
    all_gather x1, waiting for transfers between devices, hubs_edit(): o_now = all_gather(field_in, 'seq')  182 us
    ppermute x16, waiting for transfers between devices, shifted(): return lax.ppermute(block, axis, route)  143 us
    all_to_all x1, blocking collectives, body(): lax.all_to_all(hidden, FSDP, split_axis=1, concat_axis=0, tiled=True)  112 us
    ppermute x16, starting transfers between devices, shifted(): return lax.ppermute(block, axis, route)  93.4 us
    all_gather x1, waiting for transfers between devices, body(): lax.all_gather(all_grad, FSDP, axis=0, tiled=True)  53.9 us
    unnamed x36, local copies, waits for them, and re-layouts  51.9 us
    dot_general x4, matrix products, attend_group(): jnp.einsum('rhk,rhd->kd', dscores, qgrp, preferred_element_type=jnp.float32)  51.8 us
  transfers between devices with their start and end apart: 20, of which 12 were waited for; matrix products, arithmetic and copies ran while one was open for 3% of the time, Pallas kernels for 0%

profile of v1, /device:TPU:1, one launch (start us, length us, event | category | flops | bytes accessed | tf_op | source)
XLA Modules:
  0.0 1101.0 jit_solution(3516511837866165120)
XLA Ops:
  10.0 42.4 %all-gather.6.cloned.1.call-done = bf16[1024,1024]{1,0:T(8,128)(2,1)} async-done(((bf16[512,1024]{1,0:T(8,128)(2,1)}), bf16[1024,1024]{1,0:T(8,128)(2,1)}) %all-gather.6.cloned.1.call-update) | async-done | bytes 2097168 | tf_op jit(solution)/shard_map/all_gather | solution.py:20
  52.5 175.5 %all-gather.8.cloned.1.call-done = bf16[8192,1024]{1,0:T(8,128)(2,1)} async-done(((bf16[1024,1024]{1,0:T(8,128)(2,1)}), bf16[8192,1024]{1,0:T(8,128)(2,1)}) %all-gather.8.cloned.1.call-update) | async-done | bytes 16777232 | tf_op jit(solution)/shard_map/all_gather | solution.py:20
  228.0 8.1 fusion.100
  245.0 5.8 collective-permute-start.2
  272.2 15.9 %collective-permute-done.2 = bf16[128,1024]{1,0:T(8,128)(2,1)S(1)} collective-permute-done((bf16[128,1024]{1,0:T(8,128)(2,1)S(1)}, bf16[128,1024]{1,0:T(8,128)(2,1)S(1)}, u32[]{:S(2)}, u32[]{:S(2)}) %collective-permute-start.2) | collective-permute-done | bytes 262176 | tf_op jit(solution)/shard_map/ppermute | solution.py:27
  290.1 26.5 %collective-permute-done.3 = bf16[128,1024]{1,0:T(8,128)(2,1)S(1)} collective-permute-done((bf16[128,1024]{1,0:T(8,128)(2,1)S(1)}, bf16[128,1024]{1,0:T(8,128)(2,1)S(1)}, u32[]{:S(2)}, u32[]{:S(2)}) %collective-permute-start.3) | collective-permute-done | bytes 262176 | tf_op jit(solution)/shard_map/ppermute | solution.py:27
  323.6 181.8 %while.17 = (s32[]{:T(128)}, bf16[4,128,8,128]{3,1,2,0:T(8,128)(2,1)}, bf16[4,128,8,128]{3,1,2,0:T(8,128)(2,1)}, f32[4,1152,128]{1,2,0:T(8,128)}, f32[4,1152,128...) while((s32[]{:T(128)}, ...), condition=%wide.region_4.5_spmd.clone, body=%wide.region_0.4_spmd.clone.sunk | while | flops 2449958400 | bytes 52865284 | solution.py:68
  328.8 5.8 exponential_reduce_fusion.2
  334.6 12.6 %fusion.170 = bf16[4,128,8,128]{3,1,2,0:T(8,128)(2,1)} fusion(bf16[4,128,8,128]{3,1,2,0:T(8,128)(2,1)} %get-tuple-element.262, s32[]{:T(128)S(6)} %copy.95, f32[128,8,1152]{2,0,1:T(8,128)} %fusion.169, bf16[4,1152,128]{2,1,0:T(8,128)(2,1)} %get-tuple-element.279, f32[128,8,1152]{2,0,1:T(8,128)} %get-tuple-element.246, f32[128,8]{0,1:T(8,128)} %get-tuple-element.245), kind=kOutput, calls=%fused_computation.28.clone.1 | convolution fusion | flops 310380672 | bytes 19440640 | tf_op jit(solution)/shard_map/while/body/eval_jaxpr/rhk,kd->rhd/dot_general | solution.py:51
  347.2 12.9 %fusion.171 = f32[4,1152,128]{1,2,0:T(8,128)} fusion(f32[4,1152,128]{1,2,0:T(8,128)} %get-tuple-element.263, s32[]{:T(128)S(6)} %copy.95, f32[128,8,1152]{2,0,1:T(8,128)} %fusion.169, bf16[4,128,8,128]{1,3,2,0:T(8,128)(2,1)} %get-tuple-element.278, f32[128,8,1152]{2,0,1:T(8,128)} %get-tuple-element.246, f32[128,8]{0,1:T(8,128)} %get-tuple-element.245), kind=kOutput, calls=%fused_computation.17.clone.1 | convolution fusion | flops 310249600 | bytes 19735552 | tf_op jit(solution)/shard_map/while/body/eval_jaxpr/rhk,rhd->kd/dot_general | solution.py:54
  374.1 5.8 exponential_reduce_fusion.2
  379.9 12.6 %fusion.170 = bf16[4,128,8,128]{3,1,2,0:T(8,128)(2,1)} fusion(bf16[4,128,8,128]{3,1,2,0:T(8,128)(2,1)} %get-tuple-element.262, s32[]{:T(128)S(6)} %copy.95, f32[128,8,1152]{2,0,1:T(8,128)} %fusion.169, bf16[4,1152,128]{2,1,0:T(8,128)(2,1)} %get-tuple-element.279, f32[128,8,1152]{2,0,1:T(8,128)} %get-tuple-element.246, f32[128,8]{0,1:T(8,128)} %get-tuple-element.245), kind=kOutput, calls=%fused_computation.28.clone.1 | convolution fusion | flops 310380672 | bytes 19440640 | tf_op jit(solution)/shard_map/while/body/eval_jaxpr/rhk,kd->rhd/dot_general | solution.py:51
  392.4 12.9 %fusion.171 = f32[4,1152,128]{1,2,0:T(8,128)} fusion(f32[4,1152,128]{1,2,0:T(8,128)} %get-tuple-element.263, s32[]{:T(128)S(6)} %copy.95, f32[128,8,1152]{2,0,1:T(8,128)} %fusion.169, bf16[4,128,8,128]{1,3,2,0:T(8,128)(2,1)} %get-tuple-element.278, f32[128,8,1152]{2,0,1:T(8,128)} %get-tuple-element.246, f32[128,8]{0,1:T(8,128)} %get-tuple-element.245), kind=kOutput, calls=%fused_computation.17.clone.1 | convolution fusion | flops 310249600 | bytes 19735552 | tf_op jit(solution)/shard_map/while/body/eval_jaxpr/rhk,rhd->kd/dot_general | solution.py:54
  419.4 5.8 exponential_reduce_fusion.2
  425.1 12.6 %fusion.170 = bf16[4,128,8,128]{3,1,2,0:T(8,128)(2,1)} fusion(bf16[4,128,8,128]{3,1,2,0:T(8,128)(2,1)} %get-tuple-element.262, s32[]{:T(128)S(6)} %copy.95, f32[128,8,1152]{2,0,1:T(8,128)} %fusion.169, bf16[4,1152,128]{2,1,0:T(8,128)(2,1)} %get-tuple-element.279, f32[128,8,1152]{2,0,1:T(8,128)} %get-tuple-element.246, f32[128,8]{0,1:T(8,128)} %get-tuple-element.245), kind=kOutput, calls=%fused_computation.28.clone.1 | convolution fusion | flops 310380672 | bytes 19440640 | tf_op jit(solution)/shard_map/while/body/eval_jaxpr/rhk,kd->rhd/dot_general | solution.py:51
  437.8 13.0 %fusion.171 = f32[4,1152,128]{1,2,0:T(8,128)} fusion(f32[4,1152,128]{1,2,0:T(8,128)} %get-tuple-element.263, s32[]{:T(128)S(6)} %copy.95, f32[128,8,1152]{2,0,1:T(8,128)} %fusion.169, bf16[4,128,8,128]{1,3,2,0:T(8,128)(2,1)} %get-tuple-element.278, f32[128,8,1152]{2,0,1:T(8,128)} %get-tuple-element.246, f32[128,8]{0,1:T(8,128)} %get-tuple-element.245), kind=kOutput, calls=%fused_computation.17.clone.1 | convolution fusion | flops 310249600 | bytes 19735552 | tf_op jit(solution)/shard_map/while/body/eval_jaxpr/rhk,rhd->kd/dot_general | solution.py:54
  464.8 5.8 exponential_reduce_fusion.2
  470.5 12.6 %fusion.170 = bf16[4,128,8,128]{3,1,2,0:T(8,128)(2,1)} fusion(bf16[4,128,8,128]{3,1,2,0:T(8,128)(2,1)} %get-tuple-element.262, s32[]{:T(128)S(6)} %copy.95, f32[128,8,1152]{2,0,1:T(8,128)} %fusion.169, bf16[4,1152,128]{2,1,0:T(8,128)(2,1)} %get-tuple-element.279, f32[128,8,1152]{2,0,1:T(8,128)} %get-tuple-element.246, f32[128,8]{0,1:T(8,128)} %get-tuple-element.245), kind=kOutput, calls=%fused_computation.28.clone.1 | convolution fusion | flops 310380672 | bytes 19440640 | tf_op jit(solution)/shard_map/while/body/eval_jaxpr/rhk,kd->rhd/dot_general | solution.py:51
  483.1 12.9 %fusion.171 = f32[4,1152,128]{1,2,0:T(8,128)} fusion(f32[4,1152,128]{1,2,0:T(8,128)} %get-tuple-element.263, s32[]{:T(128)S(6)} %copy.95, f32[128,8,1152]{2,0,1:T(8,128)} %fusion.169, bf16[4,128,8,128]{1,3,2,0:T(8,128)(2,1)} %get-tuple-element.278, f32[128,8,1152]{2,0,1:T(8,128)} %get-tuple-element.246, f32[128,8]{0,1:T(8,128)} %get-tuple-element.245), kind=kOutput, calls=%fused_computation.17.clone.1 | convolution fusion | flops 310249600 | bytes 19735552 | tf_op jit(solution)/shard_map/while/body/eval_jaxpr/rhk,rhd->kd/dot_general | solution.py:54
  507.4 14.3 %collective-permute-start.8 = (f32[128,1024]{0,1:T(8,128)S(1)}, f32[128,1024]{0,1:T(8,128)S(1)}, u32[]{:S(2)}, u32[]{:S(2)}) collective-permute-start(f32[128,1024]{0,1:T(8,128)S(1)} %get-tuple-element.158), channel_id=1, source_target_pairs={{1,0},{2,1},{3,2},{4,3},{5,4},{6,5},{7,6},{8,7},{9,8},{10,9},{11,1... | collective-permute-start | bytes 1572872 | tf_op jit(solution)/shard_map/ppermute | solution.py:27
  541.1 23.3 %collective-permute-start.15 = (f32[128,1024]{0,1:T(8,128)S(1)}, f32[128,1024]{0,1:T(8,128)S(1)}, u32[]{:S(2)}, u32[]{:S(2)}) collective-permute-start(f32[128,1024]{0,1:T(8,128)S(1)} %get-tuple-element.164), channel_id=1, source_target_pairs={{8,0},{9,1},{10,2},{11,3},{12,4},{13,5},{14,6},{15,7},{16,8},{17,9... | collective-permute-start | bytes 1572872 | tf_op jit(solution)/shard_map/ppermute | solution.py:27
  570.0 9.4 collective-permute-done.11
  579.4 16.6 %collective-permute-done.12 = f32[128,1024]{0,1:T(8,128)S(1)} collective-permute-done((f32[128,1024]{0,1:T(8,128)S(1)}, f32[128,1024]{0,1:T(8,128)S(1)}, u32[]{:S(2)}, u32[]{:S(2)}) %collective-permute-start.12) | collective-permute-done | bytes 524320 | tf_op jit(solution)/shard_map/ppermute | solution.py:27
  596.0 58.5 %collective-permute-done.13 = f32[128,1024]{0,1:T(8,128)S(1)} collective-permute-done((f32[128,1024]{0,1:T(8,128)S(1)}, f32[128,1024]{0,1:T(8,128)S(1)}, u32[]{:S(2)}, u32[]{:S(2)}) %collective-permute-start.13) | collective-permute-done | bytes 524320 | tf_op jit(solution)/shard_map/ppermute | solution.py:27
  654.5 10.3 collective-permute-done.14
  670.8 112.4 %all_to_all.19 = bf16[128,16,512]{0,2,1:T(8,128)(2,1)} all-to-all(bf16[128,16,512]{0,2,1:T(8,128)(2,1)} %bitcast.174), channel_id=1, replica_groups=mesh['seq'=16,'fsdp_0'=8,'fsdp_1'=2] {'fsdp_0','fsdp_1'}, dimensions={1} | all-to-all | bytes 4194304 | tf_op jit(solution)/shard_map/all_to_all | solution.py:85
  787.1 53.9 %all-gather.10.cloned.1.call-done = bf16[2048,1024]{0,1:T(8,128)(2,1)} async-done(((bf16[128,1024]{0,1:T(8,128)(2,1)}), bf16[2048,1024]{0,1:T(8,128)(2,1)}) %all-gather.10.cloned.1.call-update) | async-done | bytes 4194320 | tf_op jit(solution)/shard_map/all_gather | solution.py:116
  841.0 6.5 convolution_bitcast_fusion.2
  853.1 13.9 %convolution_convert_fusion.1 = bf16[128,8192]{1,0:T(8,128)(2,1)} fusion(bf16[8192,1024]{1,0:T(8,128)(2,1)} %all-gather.8.cloned.1.call-done, f32[128,1024]{0,1:T(8,128)} %copy-done.6, f32[128,1024]{0,1:T(8,128)} %copy-done.7, f32[128,1024]{0,1:T(8,128)} %copy-done.5, f32[128,1024]{0,1:T(8,128)} %copy-done.4, f32[128,1024]{0,1:T(8,128)} %copy-done.3, ...), kind=kOutput, calls=%fused_computation.84 | convolution fusion | flops 2150891520 | bytes 27787272 | tf_op jit(solution)/shard_map/dot_general | solution.py:111
  867.1 181.8 %all-gather.12.cloned.1.call-done = f32[8192,1024]{0,1:T(8,128)} async-done(((f32[512,1024]{0,1:T(8,128)}), f32[8192,1024]{0,1:T(8,128)}) %all-gather.12.cloned.1.call-update) | async-done | bytes 33554448 | tf_op jit(solution)/shard_map/all_gather | solution.py:122
  1048.9 35.1 %copy.70 = f32[128,8,16,512]{3,2,1,0:T(8,128)S(1)} copy(f32[128,8,16,512]{3,1,2,0:T(8,128)} %bitcast.165) | data formatting | bytes 67108864
  1084.0 8.3 bitcast_reduce_fusion
  (98 shorter events, 141.9 us)
Async XLA Ops:
  7.2 1.2 copy-start.9
  7.2 45.2 %all-gather.6.cloned.1.call-start = ((), (), s32[]{:S(2)}) async-start(), calls=%async_computation.1 | async-start | bytes 3145728 | tf_op jit(solution)/shard_map/all_gather | solution.py:20
  10.0 218.0 %copy-start.1 = (bf16[128,8192]{1,0:T(8,128)(2,1)S(1)}, bf16[128,8192]{1,0:T(8,128)(2,1)}, u32[]{:S(2)}) copy-start(bf16[128,8192]{1,0:T(8,128)(2,1)} %param.7) | copy-start | bytes 6291460
  10.0 218.0 %all-gather.8.cloned.1.call-start = ((), (), s32[]{:S(2)}) async-start(), calls=%async_computation.2 | async-start | bytes 18874368 | tf_op jit(solution)/shard_map/all_gather | solution.py:20
  52.4 788.6 %all-gather.10.cloned.1.call-start = ((), (), s32[]{:S(2)}) async-start(), calls=%async_computation.3 | async-start | bytes 4456448 | tf_op jit(solution)/shard_map/all_gather | solution.py:116
  236.1 26.5 %collective-permute-start = (bf16[128,1024]{1,0:T(8,128)(2,1)S(1)}, bf16[128,1024]{1,0:T(8,128)(2,1)}, u32[]{:S(2)}, u32[]{:S(2)}) collective-permute-start(bf16[128,1024]{1,0:T(8,128)(2,1)S(1)} %fusion.100), channel_id=1, source_target_pairs={{0,8},{1,9},{2,10},{3,11},{4,12},{5,13},{6,14},{7,15},{8,16},{9,17... | collective-permute-start | bytes 786440 | tf_op jit(solution)/shard_map/ppermute | solution.py:27
  240.8 26.8 %collective-permute-start.1 = (bf16[128,1024]{1,0:T(8,128)(2,1)S(1)}, bf16[128,1024]{1,0:T(8,128)(2,1)}, u32[]{:S(2)}, u32[]{:S(2)}) collective-permute-start(bf16[128,1024]{1,0:T(8,128)(2,1)S(1)} %fusion.100), channel_id=1, source_target_pairs={{0,7},{1,8},{2,9},{3,10},{4,11},{5,12},{6,13},{7,14},{8,15},{9,16}... | collective-permute-start | bytes 786440 | tf_op jit(solution)/shard_map/ppermute | solution.py:27
  245.0 43.2 %collective-permute-start.2 = (bf16[128,1024]{1,0:T(8,128)(2,1)S(1)}, bf16[128,1024]{1,0:T(8,128)(2,1)S(1)}, u32[]{:S(2)}, u32[]{:S(2)}) collective-permute-start(bf16[128,1024]{1,0:T(8,128)(2,1)S(1)} %fusion.100), channel_id=1, source_target_pairs={{0,6},{1,7},{2,8},{3,9},{4,10},{5,11},{6,12},{7,13},{8,14},{9,15},... | collective-permute-start | bytes 786440 | tf_op jit(solution)/shard_map/ppermute | solution.py:27
  255.4 66.2 %collective-permute-start.7 = (bf16[128,1024]{1,0:T(8,128)(2,1)S(1)}, bf16[128,1024]{1,0:T(8,128)(2,1)S(1)}, u32[]{:S(2)}, u32[]{:S(2)}) collective-permute-start(bf16[128,1024]{1,0:T(8,128)(2,1)S(1)} %fusion.100), channel_id=1, source_target_pairs={{0,1},{1,2},{2,3},{3,4},{4,5},{5,6},{6,7},{7,8},{8,9},{9,10},{10,1... | collective-permute-start | bytes 786440 | tf_op jit(solution)/shard_map/ppermute | solution.py:27
  260.7 60.9 %collective-permute-start.6 = (bf16[128,1024]{1,0:T(8,128)(2,1)S(1)}, bf16[128,1024]{1,0:T(8,128)(2,1)S(1)}, u32[]{:S(2)}, u32[]{:S(2)}) collective-permute-start(bf16[128,1024]{1,0:T(8,128)(2,1)S(1)} %fusion.100), channel_id=1, source_target_pairs={{0,2},{1,3},{2,4},{3,5},{4,6},{5,7},{6,8},{7,9},{8,10},{9,11},{10,... | collective-permute-start | bytes 786440 | tf_op jit(solution)/shard_map/ppermute | solution.py:27
  262.6 54.0 %collective-permute-start.3 = (bf16[128,1024]{1,0:T(8,128)(2,1)S(1)}, bf16[128,1024]{1,0:T(8,128)(2,1)S(1)}, u32[]{:S(2)}, u32[]{:S(2)}) collective-permute-start(bf16[128,1024]{1,0:T(8,128)(2,1)S(1)} %fusion.100), channel_id=1, source_target_pairs={{0,5},{1,6},{2,7},{3,8},{4,9},{5,10},{6,11},{7,12},{8,13},{9,14},{... | collective-permute-start | bytes 786440 | tf_op jit(solution)/shard_map/ppermute | solution.py:27
  267.6 49.0 %collective-permute-start.4 = (bf16[128,1024]{1,0:T(8,128)(2,1)S(1)}, bf16[128,1024]{1,0:T(8,128)(2,1)S(1)}, u32[]{:S(2)}, u32[]{:S(2)}) collective-permute-start(bf16[128,1024]{1,0:T(8,128)(2,1)S(1)} %fusion.100), channel_id=1, source_target_pairs={{0,4},{1,5},{2,6},{3,7},{4,8},{5,9},{6,10},{7,11},{8,12},{9,13},{1... | collective-permute-start | bytes 786440 | tf_op jit(solution)/shard_map/ppermute | solution.py:27
  288.2 33.4 %collective-permute-start.5 = (bf16[128,1024]{1,0:T(8,128)(2,1)S(1)}, bf16[128,1024]{1,0:T(8,128)(2,1)S(1)}, u32[]{:S(2)}, u32[]{:S(2)}) collective-permute-start(bf16[128,1024]{1,0:T(8,128)(2,1)S(1)} %fusion.100), channel_id=1, source_target_pairs={{0,3},{1,4},{2,5},{3,6},{4,7},{5,8},{6,9},{7,10},{8,11},{9,12},{10... | collective-permute-start | bytes 786440 | tf_op jit(solution)/shard_map/ppermute | solution.py:27
  505.4 160.3 %copy-start = (f32[4,1152,128]{1,2,0:T(8,128)S(1)}, f32[4,1152,128]{1,2,0:T(8,128)}, u32[]{:S(2)}) copy-start(f32[4,1152,128]{1,2,0:T(8,128)} %get-tuple-element.61) | copy-start | bytes 7077892
  507.4 29.3 %collective-permute-start.8 = (f32[128,1024]{0,1:T(8,128)S(1)}, f32[128,1024]{0,1:T(8,128)S(1)}, u32[]{:S(2)}, u32[]{:S(2)}) collective-permute-start(f32[128,1024]{0,1:T(8,128)S(1)} %get-tuple-element.158), channel_id=1, source_target_pairs={{1,0},{2,1},{3,2},{4,3},{5,4},{6,5},{7,6},{8,7},{9,8},{10,9},{11,1... | collective-permute-start | bytes 1572872 | tf_op jit(solution)/shard_map/ppermute | solution.py:27
  521.7 19.4 %collective-permute-start.9 = (f32[128,1024]{0,1:T(8,128)S(1)}, f32[128,1024]{0,1:T(8,128)S(1)}, u32[]{:S(2)}, u32[]{:S(2)}) collective-permute-start(f32[128,1024]{0,1:T(8,128)S(1)} %get-tuple-element.159), channel_id=1, source_target_pairs={{2,0},{3,1},{4,2},{5,3},{6,4},{7,5},{8,6},{9,7},{10,8},{11,9},{12,... | collective-permute-start | bytes 1572872 | tf_op jit(solution)/shard_map/ppermute | solution.py:27
  526.4 38.0 %collective-permute-start.10 = (f32[128,1024]{0,1:T(8,128)S(1)}, f32[128,1024]{0,1:T(8,128)S(1)}, u32[]{:S(2)}, u32[]{:S(2)}) collective-permute-start(f32[128,1024]{0,1:T(8,128)S(1)} %get-tuple-element.160), channel_id=1, source_target_pairs={{3,0},{4,1},{5,2},{6,3},{7,4},{8,5},{9,6},{10,7},{11,8},{12,9},{13... | collective-permute-start | bytes 1572872 | tf_op jit(solution)/shard_map/ppermute | solution.py:27
  531.1 48.3 %collective-permute-start.11 = (f32[128,1024]{0,1:T(8,128)S(1)}, f32[128,1024]{0,1:T(8,128)S(1)}, u32[]{:S(2)}, u32[]{:S(2)}) collective-permute-start(f32[128,1024]{0,1:T(8,128)S(1)} %get-tuple-element.161), channel_id=1, source_target_pairs={{4,0},{5,1},{6,2},{7,3},{8,4},{9,5},{10,6},{11,7},{12,8},{13,9},{1... | collective-permute-start | bytes 1572872 | tf_op jit(solution)/shard_map/ppermute | solution.py:27
  534.7 61.3 %collective-permute-start.12 = (f32[128,1024]{0,1:T(8,128)S(1)}, f32[128,1024]{0,1:T(8,128)S(1)}, u32[]{:S(2)}, u32[]{:S(2)}) collective-permute-start(f32[128,1024]{0,1:T(8,128)S(1)} %get-tuple-element.162), channel_id=1, source_target_pairs={{5,0},{6,1},{7,2},{8,3},{9,4},{10,5},{11,6},{12,7},{13,8},{14,9},{... | collective-permute-start | bytes 1572872 | tf_op jit(solution)/shard_map/ppermute | solution.py:27
  536.6 117.9 %collective-permute-start.13 = (f32[128,1024]{0,1:T(8,128)S(1)}, f32[128,1024]{0,1:T(8,128)S(1)}, u32[]{:S(2)}, u32[]{:S(2)}) collective-permute-start(f32[128,1024]{0,1:T(8,128)S(1)} %get-tuple-element.163), channel_id=1, source_target_pairs={{6,0},{7,1},{8,2},{9,3},{10,4},{11,5},{12,6},{13,7},{14,8},{15,9},... | collective-permute-start | bytes 1572872 | tf_op jit(solution)/shard_map/ppermute | solution.py:27
  541.1 113.4 %collective-permute-start.15 = (f32[128,1024]{0,1:T(8,128)S(1)}, f32[128,1024]{0,1:T(8,128)S(1)}, u32[]{:S(2)}, u32[]{:S(2)}) collective-permute-start(f32[128,1024]{0,1:T(8,128)S(1)} %get-tuple-element.164), channel_id=1, source_target_pairs={{8,0},{9,1},{10,2},{11,3},{12,4},{13,5},{14,6},{15,7},{16,8},{17,9... | collective-permute-start | bytes 1572872 | tf_op jit(solution)/shard_map/ppermute | solution.py:27
  564.4 100.4 %copy-start.2 = (f32[128,1024]{0,1:T(8,128)}, f32[128,1024]{0,1:T(8,128)S(1)}, u32[]{:S(2)}) copy-start(f32[128,1024]{0,1:T(8,128)S(1)} %collective-permute-done.10) | copy-start | bytes 1572868
  564.4 100.4 %collective-permute-start.14 = (f32[128,1024]{0,1:T(8,128)S(1)}, f32[128,1024]{0,1:T(8,128)S(1)}, u32[]{:S(2)}, u32[]{:S(2)}) collective-permute-start(f32[128,1024]{0,1:T(8,128)S(1)} %get-tuple-element.165), channel_id=1, source_target_pairs={{7,0},{8,1},{9,2},{10,3},{11,4},{12,5},{13,6},{14,7},{15,8},{16,9}... | collective-permute-start | bytes 1572872 | tf_op jit(solution)/shard_map/ppermute | solution.py:27
  579.4 85.4 %copy-start.3 = (f32[128,1024]{0,1:T(8,128)}, f32[128,1024]{0,1:T(8,128)S(1)}, u32[]{:S(2)}) copy-start(f32[128,1024]{0,1:T(8,128)S(1)} %collective-permute-done.11) | copy-start | bytes 1572868
  596.0 68.8 %copy-start.4 = (f32[128,1024]{0,1:T(8,128)}, f32[128,1024]{0,1:T(8,128)S(1)}, u32[]{:S(2)}) copy-start(f32[128,1024]{0,1:T(8,128)S(1)} %collective-permute-done.12) | copy-start | bytes 1572868
  654.5 10.3 copy-start.5
  654.5 10.3 copy-start.6
  664.8 0.8 copy-start.7
  666.6 382.3 %all-gather.12.cloned.1.call-start = ((), (), s32[]{:S(2)}) async-start(), calls=%async_computation.4 | async-start | bytes 35651584 | tf_op jit(solution)/shard_map/all_gather | solution.py:122
  847.6 3.4 copy-start.8
Sparse Core Ops, SparseCore 0:
  10.4 41.9 all-gather.5
  54.2 173.7 all-gather.7
  666.8 174.2 all-gather.9
  847.7 201.1 all-gather.11
